TPU v7x, 32 devices: a whole 2x2x4 slice. The times are simulated.
32 devices in a mesh: seq: 2 (over x), fsdp: 16 (over z, y, core).
Axes of the slice: x: 2, y: 2, z: 4, core: 2. Of those that a mesh axis runs over, the one named last changes fastest.
Arguments:
- frames_in: float32 [16, 256, 768], P('fsdp', 'seq'), may hold values from -6 to 6
- cotangent: float32 [16, 256, 768], P('fsdp', 'seq'), may hold values from -6 to 6
- first_gain: bfloat16 [1, 768], P(None, 'fsdp'), may hold values from 0.099609375 to 1.8984375
- first_bias: bfloat16 [1, 768], P(None, 'fsdp'), may hold values from -3 to 3
- query_weight: bfloat16 [1, 768, 768], P(None, 'fsdp'), may hold values from -0.21875 to 0.21875
- query_bias: bfloat16 [1, 768], P(None, 'fsdp'), may hold values from -3 to 3
- key_weight: bfloat16 [1, 768, 768], P(None, 'fsdp'), may hold values from -0.21875 to 0.21875
- value_weight: bfloat16 [1, 768, 768], P(None, 'fsdp'), may hold values from -0.21875 to 0.21875
- value_bias: bfloat16 [1, 768], P(None, 'fsdp'), may hold values from -3 to 3
- out_weight: bfloat16 [1, 768, 768], P(None, 'fsdp'), may hold values from -3.5 to 3.5
- out_bias: bfloat16 [1, 768], P(None, 'fsdp'), may hold values from -3 to 3
- second_gain: bfloat16 [1, 768], P(None, 'fsdp'), may hold values from 0.099609375 to 1.8984375
- second_bias: bfloat16 [1, 768], P(None, 'fsdp'), may hold values from -3 to 3
- up_weight: bfloat16 [1, 768, 3072], P(None, 'fsdp'), may hold values from -0.21875 to 0.21875
- up_bias: bfloat16 [1, 3072], P(None, 'fsdp'), may hold values from -3 to 3
- down_weight: bfloat16 [1, 3072, 768], P(None, 'fsdp'), may hold values from -0.109375 to 0.109375
- down_bias: bfloat16 [1, 768], P(None, 'fsdp'), may hold values from -3 to 3
Outputs:
- outputs: float32 [16, 256, 768], P('fsdp', 'seq')
- input_gradient: float32 [16, 256, 768], P('fsdp', 'seq')
- first_gain_gradient: float32 [1, 768], P(None, 'fsdp')
- first_bias_gradient: float32 [1, 768], P(None, 'fsdp')
- query_weight_gradient: float32 [1, 768, 768], P(None, 'fsdp')
- query_bias_gradient: float32 [1, 768], P(None, 'fsdp')
- key_weight_gradient: float32 [1, 768, 768], P(None, 'fsdp')
- value_weight_gradient: float32 [1, 768, 768], P(None, 'fsdp')
- value_bias_gradient: float32 [1, 768], P(None, 'fsdp')
- out_weight_gradient: float32 [1, 768, 768], P(None, 'fsdp')
- out_bias_gradient: float32 [1, 768], P(None, 'fsdp')
- second_gain_gradient: float32 [1, 768], P(None, 'fsdp')
- second_bias_gradient: float32 [1, 768], P(None, 'fsdp')
- up_weight_gradient: float32 [1, 768, 3072], P(None, 'fsdp')
- up_bias_gradient: float32 [1, 3072], P(None, 'fsdp')
- down_weight_gradient: float32 [1, 3072, 768], P(None, 'fsdp')
- down_bias_gradient: float32 [1, 768], P(None, 'fsdp')
All inputs are finite; a program needn't handle non-finite values.
Results may differ from a plain program's by a relative error of at most 0.012.
The roundings to bfloat16 on the way count: a program that leaves them out, or rounds other values in their place, can miss the bound.
Values may be sent and summed in bfloat16 or wider, within the bound.
A program may use at most 128 MiB of HBM per device.

v0:
```python
import jax
import jax.numpy as jnp
from jax import lax
from jax.sharding import PartitionSpec as P

HEAD_DIM = 64
EPSILON = 1e-05
ROOT_HALF = 0.7071067811865476
INV_ROOT_TAU = 0.3989422804014327


def matmul(left, right):
    return jnp.dot(left, right, preferred_element_type=jnp.float32)


def contract_rows(left, right):
    return lax.dot_general(
        left, right, (((0,), (0,)), ((), ())), preferred_element_type=jnp.float32
    )


def contract_cols(left, right):
    return lax.dot_general(
        left, right, (((1,), (1,)), ((), ())), preferred_element_type=jnp.float32
    )


def layer_norm(residual, gain, offset):
    centre = residual - jnp.mean(residual, axis=-1, keepdims=True)
    inv_std = lax.rsqrt(jnp.mean(centre * centre, axis=-1, keepdims=True) + EPSILON)
    normed = centre * inv_std
    return (normed * gain.astype(jnp.float32) + offset.astype(jnp.float32), normed, inv_std)


def norm_grad(upstream, normed, inv_std, gain):
    scaled = upstream * gain.astype(jnp.float32)
    spread = scaled - jnp.mean(scaled, axis=-1, keepdims=True)
    return (spread - normed * jnp.mean(scaled * normed, axis=-1, keepdims=True)) * inv_std


def gelu_exact(pre_act):
    return 0.5 * pre_act * (1.0 + lax.erf(pre_act * ROOT_HALF))


def gelu_slope(pre_act):
    return (
        0.5 * (1.0 + lax.erf(pre_act * ROOT_HALF))
        + pre_act * jnp.exp(-0.5 * pre_act * pre_act) * INV_ROOT_TAU
    )


def split_heads(rows):
    return rows.reshape(rows.shape[0], rows.shape[1] // HEAD_DIM, HEAD_DIM)


def attend(query_rows, key_rows, value_rows):
    score_scale = HEAD_DIM ** (-0.5)
    query_heads = split_heads(query_rows)
    key_heads = split_heads(key_rows)
    value_heads = split_heads(value_rows)
    scores = (
        jnp.einsum("qhd,khd->hqk", query_heads, key_heads, preferred_element_type=jnp.float32)
        * score_scale
    )
    row_top = jnp.max(scores, axis=-1, keepdims=True)
    log_total = row_top + jnp.log(jnp.sum(jnp.exp(scores - row_top), axis=-1, keepdims=True))
    weights_low = jnp.exp(scores - log_total).astype(jnp.bfloat16)
    context = jnp.einsum(
        "hqk,khd->qhd", weights_low, value_heads, preferred_element_type=jnp.float32
    )
    return (context.reshape(query_rows.shape).astype(jnp.bfloat16), log_total)


def attend_back(query_rows, key_rows, value_rows, log_total, context_gradient):
    score_scale = HEAD_DIM ** (-0.5)
    row_shape = query_rows.shape
    query_heads = split_heads(query_rows)
    key_heads = split_heads(key_rows)
    value_heads = split_heads(value_rows)
    gradient_heads = split_heads(context_gradient)
    scores = (
        jnp.einsum("qhd,khd->hqk", query_heads, key_heads, preferred_element_type=jnp.float32)
        * score_scale
    )
    weights = jnp.exp(scores - log_total)
    weights_low = weights.astype(jnp.bfloat16)
    value_gradient = jnp.einsum(
        "hqk,qhd->khd", weights_low, gradient_heads, preferred_element_type=jnp.float32
    )
    prob_gradient = jnp.einsum(
        "qhd,khd->hqk", gradient_heads, value_heads, preferred_element_type=jnp.float32
    )
    score_gradient = (
        weights
        * (prob_gradient - jnp.sum(weights * prob_gradient, axis=-1, keepdims=True))
        * score_scale
    ).astype(jnp.bfloat16)
    query_gradient = jnp.einsum(
        "hqk,khd->qhd", score_gradient, key_heads, preferred_element_type=jnp.float32
    )
    key_gradient = jnp.einsum(
        "hqk,qhd->khd", score_gradient, query_heads, preferred_element_type=jnp.float32
    )
    return jnp.stack(
        [
            query_gradient.reshape(row_shape),
            key_gradient.reshape(row_shape),
            value_gradient.reshape(row_shape),
        ]
    ).astype(jnp.bfloat16)


def gather_layer(shards):
    return (
        lax.all_gather(shards[0], "fsdp", axis=0, tiled=True),
        lax.all_gather(shards[1], "fsdp", axis=0, tiled=True),
        lax.all_gather(shards[2], "fsdp", axis=0, tiled=True),
        lax.all_gather(shards[3], "fsdp", axis=0, tiled=True),
        lax.all_gather(shards[4], "fsdp", axis=0, tiled=True),
        lax.all_gather(shards[5], "fsdp", axis=0, tiled=True),
        lax.all_gather(shards[6], "fsdp", axis=0, tiled=True),
        lax.all_gather(shards[7], "fsdp", axis=0, tiled=True),
        lax.all_gather(shards[8], "fsdp", axis=0, tiled=True),
        lax.all_gather(shards[9], "fsdp", axis=0, tiled=True),
        lax.all_gather(shards[10], "fsdp", axis=0, tiled=True),
        lax.all_gather(shards[11], "fsdp", axis=0, tiled=True),
        lax.all_gather(shards[12], "fsdp", axis=0, tiled=True),
        lax.all_gather(shards[13], "fsdp", axis=0, tiled=True),
        lax.all_gather(shards[14], "fsdp", axis=0, tiled=True),
    )


def forward_layer(residual, params):
    hidden_wide, normed_in, inv_in = layer_norm(residual, params[0], params[1])
    hidden = hidden_wide.astype(jnp.bfloat16)
    query_rows = (matmul(hidden, params[2]) + params[3].astype(jnp.float32)).astype(jnp.bfloat16)
    key_rows = matmul(hidden, params[4]).astype(jnp.bfloat16)
    value_rows = (matmul(hidden, params[5]) + params[6].astype(jnp.float32)).astype(jnp.bfloat16)
    by_head = lax.all_to_all(
        jnp.stack([query_rows, key_rows, value_rows]),
        "seq",
        split_axis=2,
        concat_axis=1,
        tiled=True,
    )
    context_heads, log_total = attend(by_head[0], by_head[1], by_head[2])
    context = lax.all_to_all(context_heads, "seq", split_axis=0, concat_axis=1, tiled=True)
    middle = residual + matmul(context, params[7]) + params[8].astype(jnp.float32)
    mid_wide, normed_mid, inv_mid = layer_norm(middle, params[9], params[10])
    hidden_mid = mid_wide.astype(jnp.bfloat16)
    pre_act = matmul(hidden_mid, params[11]) + params[12].astype(jnp.float32)
    activated = gelu_exact(pre_act).astype(jnp.bfloat16)
    result = middle + matmul(activated, params[13]) + params[14].astype(jnp.float32)
    return (
        result,
        (
            hidden,
            normed_in,
            inv_in,
            by_head,
            log_total,
            context,
            normed_mid,
            inv_mid,
            hidden_mid,
            pre_act,
            activated,
        ),
    )


def backward_layer(upstream, stored, params):
    (
        hidden,
        normed_in,
        inv_in,
        by_head,
        log_total,
        context,
        normed_mid,
        inv_mid,
        hidden_mid,
        pre_act,
        activated,
    ) = stored
    upstream_low = upstream.astype(jnp.bfloat16)
    down_weight_gradient = contract_rows(activated, upstream_low)
    down_bias_gradient = jnp.sum(upstream, axis=0)
    pre_gradient = contract_cols(upstream_low, params[13]) * gelu_slope(pre_act)
    pre_low = pre_gradient.astype(jnp.bfloat16)
    up_weight_gradient = contract_rows(hidden_mid, pre_low)
    up_bias_gradient = jnp.sum(pre_gradient, axis=0)
    mid_hidden_gradient = contract_cols(pre_low, params[11])
    second_gain_gradient = jnp.sum(mid_hidden_gradient * normed_mid, axis=0)
    second_bias_gradient = jnp.sum(mid_hidden_gradient, axis=0)
    middle_gradient = upstream + norm_grad(mid_hidden_gradient, normed_mid, inv_mid, params[9])
    middle_low = middle_gradient.astype(jnp.bfloat16)
    out_weight_gradient = contract_rows(context, middle_low)
    out_bias_gradient = jnp.sum(middle_gradient, axis=0)
    context_gradient = contract_cols(middle_low, params[7]).astype(jnp.bfloat16)
    head_gradient = lax.all_to_all(context_gradient, "seq", split_axis=1, concat_axis=0, tiled=True)
    head_parts = attend_back(by_head[0], by_head[1], by_head[2], log_total, head_gradient)
    frame_parts = lax.all_to_all(head_parts, "seq", split_axis=1, concat_axis=2, tiled=True)
    query_gradient = frame_parts[0]
    key_gradient = frame_parts[1]
    value_gradient = frame_parts[2]
    query_weight_gradient = contract_rows(hidden, query_gradient)
    query_bias_gradient = jnp.sum(query_gradient.astype(jnp.float32), axis=0)
    key_weight_gradient = contract_rows(hidden, key_gradient)
    value_weight_gradient = contract_rows(hidden, value_gradient)
    value_bias_gradient = jnp.sum(value_gradient.astype(jnp.float32), axis=0)
    hidden_gradient = (
        contract_cols(query_gradient, params[2])
        + contract_cols(key_gradient, params[4])
        + contract_cols(value_gradient, params[5])
    )
    first_gain_gradient = jnp.sum(hidden_gradient * normed_in, axis=0)
    first_bias_gradient = jnp.sum(hidden_gradient, axis=0)
    input_gradient = middle_gradient + norm_grad(hidden_gradient, normed_in, inv_in, params[0])
    return (
        input_gradient,
        (
            first_gain_gradient,
            first_bias_gradient,
            query_weight_gradient,
            query_bias_gradient,
            key_weight_gradient,
            value_weight_gradient,
            value_bias_gradient,
            out_weight_gradient,
            out_bias_gradient,
            second_gain_gradient,
            second_bias_gradient,
            up_weight_gradient,
            up_bias_gradient,
            down_weight_gradient,
            down_bias_gradient,
        ),
    )


def reduce_gradients(gradients):
    shards = (
        lax.psum_scatter(gradients[0], "fsdp", scatter_dimension=0, tiled=True),
        lax.psum_scatter(gradients[1], "fsdp", scatter_dimension=0, tiled=True),
        lax.psum_scatter(gradients[2], "fsdp", scatter_dimension=0, tiled=True),
        lax.psum_scatter(gradients[3], "fsdp", scatter_dimension=0, tiled=True),
        lax.psum_scatter(gradients[4], "fsdp", scatter_dimension=0, tiled=True),
        lax.psum_scatter(gradients[5], "fsdp", scatter_dimension=0, tiled=True),
        lax.psum_scatter(gradients[6], "fsdp", scatter_dimension=0, tiled=True),
        lax.psum_scatter(gradients[7], "fsdp", scatter_dimension=0, tiled=True),
        lax.psum_scatter(gradients[8], "fsdp", scatter_dimension=0, tiled=True),
        lax.psum_scatter(gradients[9], "fsdp", scatter_dimension=0, tiled=True),
        lax.psum_scatter(gradients[10], "fsdp", scatter_dimension=0, tiled=True),
        lax.psum_scatter(gradients[11], "fsdp", scatter_dimension=0, tiled=True),
        lax.psum_scatter(gradients[12], "fsdp", scatter_dimension=0, tiled=True),
        lax.psum_scatter(gradients[13], "fsdp", scatter_dimension=0, tiled=True),
        lax.psum_scatter(gradients[14], "fsdp", scatter_dimension=0, tiled=True),
    )
    parts = (
        lax.psum_scatter(shards[0], "seq", scatter_dimension=0, tiled=True),
        lax.psum_scatter(shards[1], "seq", scatter_dimension=0, tiled=True),
        lax.psum_scatter(shards[2], "seq", scatter_dimension=0, tiled=True),
        lax.psum_scatter(shards[3], "seq", scatter_dimension=0, tiled=True),
        lax.psum_scatter(shards[4], "seq", scatter_dimension=0, tiled=True),
        lax.psum_scatter(shards[5], "seq", scatter_dimension=0, tiled=True),
        lax.psum_scatter(shards[6], "seq", scatter_dimension=0, tiled=True),
        lax.psum_scatter(shards[7], "seq", scatter_dimension=0, tiled=True),
        lax.psum_scatter(shards[8], "seq", scatter_dimension=0, tiled=True),
        lax.psum_scatter(shards[9], "seq", scatter_dimension=0, tiled=True),
        lax.psum_scatter(shards[10], "seq", scatter_dimension=0, tiled=True),
        lax.psum_scatter(shards[11], "seq", scatter_dimension=0, tiled=True),
        lax.psum_scatter(shards[12], "seq", scatter_dimension=0, tiled=True),
        lax.psum_scatter(shards[13], "seq", scatter_dimension=0, tiled=True),
        lax.psum_scatter(shards[14], "seq", scatter_dimension=0, tiled=True),
    )
    return (
        lax.all_gather(parts[0], "seq", axis=0, tiled=True),
        lax.all_gather(parts[1], "seq", axis=0, tiled=True),
        lax.all_gather(parts[2], "seq", axis=0, tiled=True),
        lax.all_gather(parts[3], "seq", axis=0, tiled=True),
        lax.all_gather(parts[4], "seq", axis=0, tiled=True),
        lax.all_gather(parts[5], "seq", axis=0, tiled=True),
        lax.all_gather(parts[6], "seq", axis=0, tiled=True),
        lax.all_gather(parts[7], "seq", axis=0, tiled=True),
        lax.all_gather(parts[8], "seq", axis=0, tiled=True),
        lax.all_gather(parts[9], "seq", axis=0, tiled=True),
        lax.all_gather(parts[10], "seq", axis=0, tiled=True),
        lax.all_gather(parts[11], "seq", axis=0, tiled=True),
        lax.all_gather(parts[12], "seq", axis=0, tiled=True),
        lax.all_gather(parts[13], "seq", axis=0, tiled=True),
        lax.all_gather(parts[14], "seq", axis=0, tiled=True),
    )


def on_device(
    frames_in,
    cotangent,
    first_gain,
    first_bias,
    query_weight,
    query_bias,
    key_weight,
    value_weight,
    value_bias,
    out_weight,
    out_bias,
    second_gain,
    second_bias,
    up_weight,
    up_bias,
    down_weight,
    down_bias,
):
    stacks = (
        first_gain,
        first_bias,
        query_weight,
        query_bias,
        key_weight,
        value_weight,
        value_bias,
        out_weight,
        out_bias,
        second_gain,
        second_bias,
        up_weight,
        up_bias,
        down_weight,
        down_bias,
    )
    layer_count = first_gain.shape[0]
    residual = frames_in[0]
    layer_num = 0
    params = gather_layer([stack[layer_num] for stack in stacks])
    residual, stored = forward_layer(residual, params)
    stored_all = [stored]
    gathered = [params]
    upstream = cotangent[0]
    reduced = [None] * layer_count
    for layer_num in reversed(range(layer_count)):
        params = gathered[layer_num]
        upstream, gradients = backward_layer(upstream, stored_all[layer_num], params)
        reduced[layer_num] = reduce_gradients(gradients)
    results = [residual[None], upstream[None]]
    for member in range(len(stacks)):
        results.append(jnp.stack([reduced[0][member]]))
    return tuple(results)


def solution(mesh):
    return jax.shard_map(
        on_device,
        mesh=mesh,
        in_specs=(
            P("fsdp", "seq", None),
            P("fsdp", "seq", None),
            P(None, "fsdp"),
            P(None, "fsdp"),
            P(None, "fsdp", None),
            P(None, "fsdp"),
            P(None, "fsdp", None),
            P(None, "fsdp", None),
            P(None, "fsdp"),
            P(None, "fsdp", None),
            P(None, "fsdp"),
            P(None, "fsdp"),
            P(None, "fsdp"),
            P(None, "fsdp", None),
            P(None, "fsdp"),
            P(None, "fsdp", None),
            P(None, "fsdp"),
        ),
        out_specs=(
            P("fsdp", "seq", None),
            P("fsdp", "seq", None),
            P(None, "fsdp"),
            P(None, "fsdp"),
            P(None, "fsdp", None),
            P(None, "fsdp"),
            P(None, "fsdp", None),
            P(None, "fsdp", None),
            P(None, "fsdp"),
            P(None, "fsdp", None),
            P(None, "fsdp"),
            P(None, "fsdp"),
            P(None, "fsdp"),
            P(None, "fsdp", None),
            P(None, "fsdp"),
            P(None, "fsdp", None),
            P(None, "fsdp"),
        ),
        check_vma=False,
    )
```

profile of v0, /device:TPU:0, one launch (start us, length us, event | category | flops | bytes accessed | tf_op | source)
XLA Modules:
  0.0 885.4 jit_solution(2830720401970173773)
XLA Ops:
  21.5 63.2 %all-reduce.39 = (bf16[768]{0:T(1024)(128)(2,1)S(1)}, bf16[768]{0:T(1024)(128)(2,1)S(1)}, bf16[768]{0:T(1024)(128)(2,1)S(1)}, bf16[768]{0:T(1024)(128)(2,1)S(1)}...) all-reduce(bf16[768]{0:T(1024)(128)(2,1)S(1)} %dynamic-update-slice, ...), channel_id=3, replica_groups=mesh['seq'=2,'fsdp'=16] {'fsdp'}, use_global_device_ids=true, to_apply=%add.1 | all-reduce | flops 9216 | bytes 36864
  92.5 37.9 %all-gather.22.cloned.1.call-done = bf16[1,768,768]{2,1,0:T(8,128)(2,1)} async-done(((bf16[1,48,768]{2,1,0:T(8,128)(2,1)}), bf16[1,768,768]{2,1,0:T(8,128)(2,1)}) %all-gather.22.cloned.1.call-update) | async-done | bytes 1179664 | tf_op jit(solution)/shard_map/all_gather | solution.py:117
  132.7 13.9 %all_to_all.62 = bf16[3,128,768]{1,0,2:T(4,128)(2,1)S(1)} all-to-all(bf16[3,128,768]{1,0,2:T(4,128)(2,1)S(1)} %copy.66), channel_id=1, replica_groups=mesh['seq'=2,'fsdp'=16] {'seq'}, dimensions={2} | all-to-all | bytes 1179648 | tf_op jit(solution)/shard_map/all_to_all | solution.py:139
  154.1 15.5 %all-gather.28.cloned.1.call-done = bf16[1,768,768]{2,1,0:T(8,128)(2,1)} async-done(((bf16[1,48,768]{2,1,0:T(8,128)(2,1)}), bf16[1,768,768]{2,1,0:T(8,128)(2,1)}) %all-gather.28.cloned.1.call-update) | async-done | bytes 1179664 | tf_op jit(solution)/shard_map/all_gather | solution.py:122
  171.6 52.2 %all-gather.30.cloned.1.call-done = bf16[1,768,3072]{2,1,0:T(8,128)(2,1)} async-done(((bf16[1,48,3072]{2,1,0:T(8,128)(2,1)}), bf16[1,768,3072]{2,1,0:T(8,128)(2,1)}) %all-gather.30.cloned.1.call-update) | async-done | bytes 4718608 | tf_op jit(solution)/shard_map/all_gather | solution.py:126
  228.1 49.5 %all-gather.32.cloned.1.call-done = bf16[1,3072,768]{2,1,0:T(8,128)(2,1)} async-done(((bf16[1,192,768]{2,1,0:T(8,128)(2,1)}), bf16[1,3072,768]{2,1,0:T(8,128)(2,1)}) %all-gather.32.cloned.1.call-update) | async-done | bytes 4718608 | tf_op jit(solution)/shard_map/all_gather | solution.py:128
  277.6 5.3 fusion.108
  290.6 7.5 all_to_all.63
  316.1 12.9 %all_to_all.64 = bf16[3,256,384]{2,0,1:T(4,128)(2,1)S(1)} all-to-all(bf16[3,256,384]{2,0,1:T(4,128)(2,1)S(1)} %pad_maximum_fusion), channel_id=1, replica_groups=mesh['seq'=2,'fsdp'=16] {'seq'}, dimensions={1} | all-to-all | bytes 1179648 | tf_op jit(solution)/shard_map/all_to_all | solution.py:203
  350.6 65.9 %reduce-scatter.13.cloned.1.call-done = f32[48,768]{1,0:T(8,128)} async-done(((f32[768,768]{1,0:T(8,128)}), f32[48,768]{1,0:T(8,128)}) %reduce-scatter.13.cloned.1.call-update) | async-done | bytes 147472 | tf_op jit(solution)/shard_map/reduce_scatter | solution.py:246
  420.6 62.0 %reduce-scatter.17.cloned.1.call-done = f32[48,768]{1,0:T(8,128)} async-done(((f32[768,768]{1,0:T(8,128)}), f32[48,768]{1,0:T(8,128)}) %reduce-scatter.17.cloned.1.call-update) | async-done | bytes 147472 | tf_op jit(solution)/shard_map/reduce_scatter | solution.py:248
  486.6 61.8 %reduce-scatter.21.cloned.1.call-done = f32[48,768]{1,0:T(8,128)} async-done(((f32[768,768]{1,0:T(8,128)}), f32[48,768]{1,0:T(8,128)}) %reduce-scatter.21.cloned.1.call-update) | async-done | bytes 147472 | tf_op jit(solution)/shard_map/reduce_scatter | solution.py:249
  552.7 110.2 %reduce-scatter.29.cloned.1.call-done = f32[48,3072]{1,0:T(8,128)} async-done(((f32[768,3072]{1,0:T(8,128)}), f32[48,3072]{1,0:T(8,128)}) %reduce-scatter.29.cloned.1.call-update) | async-done | bytes 589840 | tf_op jit(solution)/shard_map/reduce_scatter | solution.py:255
  665.8 62.5 %all-reduce.36 = (f32[768]{0:T(1024)S(1)}, f32[768]{0:T(1024)S(1)}, f32[768]{0:T(1024)S(1)}, f32[768]{0:T(1024)S(1)}, f32[768]{0:T(1024)S(1)}, /*index=5*/f32[76...) all-reduce(f32[768]{0:T(1024)S(1)} %get-tuple-element.19, ...), channel_id=17, replica_groups=mesh['seq'=2,'fsdp'=16] {'fsdp'}, use_global_device_ids=true, to_apply=%region_12.0.clone | all-reduce | flops 9216 | bytes 73728
  735.1 44.5 %reduce-scatter.33.cloned.1.call-done = f32[192,768]{1,0:T(8,128)} async-done(((f32[3072,768]{1,0:T(8,128)}), f32[192,768]{1,0:T(8,128)}) %reduce-scatter.33.cloned.1.call-update) | async-done | bytes 589840 | tf_op jit(solution)/shard_map/reduce_scatter | solution.py:257
  779.9 5.5 all-reduce.37
  786.4 5.6 reduce-scatter.27.cloned.1.call-done
  797.2 7.4 reduce-scatter.15.cloned.1.call-done
  809.8 7.4 reduce-scatter.19.cloned.1.call-done
  822.5 7.4 reduce-scatter.23.cloned.1.call-done
  835.1 12.3 %reduce-scatter.31.cloned.1.call-done = f32[24,3072]{1,0:T(8,128)} async-done(((f32[48,3072]{1,0:T(8,128)}), f32[24,3072]{1,0:T(8,128)}) %reduce-scatter.31.cloned.1.call-update) | async-done | bytes 294928 | tf_op jit(solution)/shard_map/reduce_scatter | solution.py:272
  847.3 9.5 %all_gather.116 = f32[48,3072]{1,0:T(8,128)S(1)} all-gather(f32[24,3072]{1,0:T(8,128)} %reduce-scatter.31.cloned.1.call-done), channel_id=1, replica_groups=mesh['seq'=2,'fsdp'=16] {'seq'}, dimensions={0}, use_global_device_ids=true | all-gather | bytes 884736 | tf_op jit(solution)/shard_map/all_gather | solution.py:289
  856.8 8.0 reduce-scatter.35.cloned.1.call-done
  864.9 9.5 %all_gather.118 = f32[192,768]{1,0:T(8,128)S(1)} all-gather(f32[96,768]{1,0:T(8,128)} %reduce-scatter.35.cloned.1.call-done), channel_id=1, replica_groups=mesh['seq'=2,'fsdp'=16] {'seq'}, dimensions={0}, use_global_device_ids=true | all-gather | bytes 884736 | tf_op jit(solution)/shard_map/all_gather | solution.py:291
  (229 shorter events, 128.0 us)
Async XLA Ops:
  7.2 78.9 %all-gather.24.cloned.1.call-start = ((), (), s32[]{:S(2)}) async-start(), calls=%async_computation.29 | async-start | bytes 1253376 | tf_op jit(solution)/shard_map/all_gather | solution.py:119
  7.9 82.9 %all-gather.26.cloned.1.call-start = ((), (), s32[]{:S(2)}) async-start(), calls=%async_computation.30 | async-start | bytes 1253376 | tf_op jit(solution)/shard_map/all_gather | solution.py:120
  8.7 121.7 %all-gather.22.cloned.1.call-start = ((), (), s32[]{:S(2)}) async-start(), calls=%async_computation.28 | async-start | bytes 1253376 | tf_op jit(solution)/shard_map/all_gather | solution.py:117
  9.4 160.2 %all-gather.28.cloned.1.call-start = ((), (), s32[]{:S(2)}) async-start(), calls=%async_computation.31 | async-start | bytes 1253376 | tf_op jit(solution)/shard_map/all_gather | solution.py:122
  10.0 213.8 %all-gather.30.cloned.1.call-start = ((), (), s32[]{:S(2)}) async-start(), calls=%async_computation.32 | async-start | bytes 5013504 | tf_op jit(solution)/shard_map/all_gather | solution.py:126
  10.6 267.0 %all-gather.32.cloned.1.call-start = ((), (), s32[]{:S(2)}) async-start(), calls=%async_computation.33 | async-start | bytes 5013504 | tf_op jit(solution)/shard_map/all_gather | solution.py:128
  150.6 19.0 %all-to-all-start.1 = ((bf16[2,128,384]{1,2,0:T(8,128)(2,1)}), bf16[2,128,384]{1,2,0:T(8,128)(2,1)S(1)}, u32[]{:S(2)}, u32[]{:S(2)}) async-start(bf16[2,128,384]{1,2,0:T(8,128)(2,1)} %copy.69), calls=%async_computation.1 | async-start | bytes 393216 | tf_op jit(solution)/shard_map/all_to_all | solution.py:147
  154.0 196.5 %reduce-scatter.25.cloned.1.call-start = ((), (), s32[]{:S(2)}) async-start(), calls=%async_computation.22 | async-start | bytes 2506752 | tf_op jit(solution)/shard_map/reduce_scatter | solution.py:251
  171.3 111.6 %copy-start.20 = (f32[128]{0:T(128)}, f32[128]{0:T(128)S(1)}, u32[]{:S(2)}) copy-start(f32[128]{0:T(128)S(1)} %broadcast_multiply_fusion.4) | copy-start | bytes 1540
  171.5 111.4 %copy-start.25 = (f32[128]{0:T(128)}, f32[128]{0:T(128)S(1)}, u32[]{:S(2)}) copy-start(f32[128]{0:T(128)S(1)} %add_rsqrt_fusion) | copy-start | bytes 1540
  288.7 127.9 %reduce-scatter.13.cloned.1.call-start = ((), (), s32[]{:S(2)}) async-start(), calls=%async_computation.16 | async-start | bytes 2506752 | tf_op jit(solution)/shard_map/reduce_scatter | solution.py:246
  332.2 150.4 %reduce-scatter.17.cloned.1.call-start = ((), (), s32[]{:S(2)}) async-start(), calls=%async_computation.18 | async-start | bytes 2506752 | tf_op jit(solution)/shard_map/reduce_scatter | solution.py:248
  334.6 213.9 %reduce-scatter.21.cloned.1.call-start = ((), (), s32[]{:S(2)}) async-start(), calls=%async_computation.20 | async-start | bytes 2506752 | tf_op jit(solution)/shard_map/reduce_scatter | solution.py:249
  336.9 326.0 %reduce-scatter.29.cloned.1.call-start = ((), (), s32[]{:S(2)}) async-start(), calls=%async_computation.24 | async-start | bytes 10027008 | tf_op jit(solution)/shard_map/reduce_scatter | solution.py:255
  343.2 436.4 %reduce-scatter.33.cloned.1.call-start = ((), (), s32[]{:S(2)}) async-start(), calls=%async_computation.26 | async-start | bytes 10027008 | tf_op jit(solution)/shard_map/reduce_scatter | solution.py:257
  349.6 442.4 %reduce-scatter.27.cloned.1.call-start = ((), (), s32[]{:S(2)}) async-start(), calls=%async_computation.23 | async-start | bytes 221184 | tf_op jit(solution)/shard_map/reduce_scatter | solution.py:268
  350.6 454.0 %reduce-scatter.15.cloned.1.call-start = ((), (), s32[]{:S(2)}) async-start(), calls=%async_computation.17 | async-start | bytes 221184 | tf_op jit(solution)/shard_map/reduce_scatter | solution.py:263
  416.6 400.6 %reduce-scatter.19.cloned.1.call-start = ((), (), s32[]{:S(2)}) async-start(), calls=%async_computation.19 | async-start | bytes 221184 | tf_op jit(solution)/shard_map/reduce_scatter | solution.py:265
  482.6 347.2 %reduce-scatter.23.cloned.1.call-start = ((), (), s32[]{:S(2)}) async-start(), calls=%async_computation.21 | async-start | bytes 221184 | tf_op jit(solution)/shard_map/reduce_scatter | solution.py:266
  548.5 298.9 %reduce-scatter.31.cloned.1.call-start = ((), (), s32[]{:S(2)}) async-start(), calls=%async_computation.25 | async-start | bytes 884736 | tf_op jit(solution)/shard_map/reduce_scatter | solution.py:272
  550.4 113.7 %copy-start.3 = (bf16[1,768,768]{2,1,0:T(8,128)(2,1)S(1)}, bf16[1,768,768]{2,1,0:T(8,128)(2,1)}, u32[]{:S(2)}) copy-start(bf16[1,768,768]{2,1,0:T(8,128)(2,1)} %all-gather.26.cloned.1.call-done) | copy-start | bytes 3538948
  550.4 113.7 %copy-start.16 = (f32[128]{0:T(128)S(1)}, f32[128]{0:T(128)}, u32[]{:S(2)}) copy-start(f32[128]{0:T(128)} %copy-done.14) | copy-start | bytes 1540
  550.4 113.7 %copy-start.19 = (f32[128]{0:T(128)S(1)}, f32[128]{0:T(128)}, u32[]{:S(2)}) copy-start(f32[128]{0:T(128)} %copy-done.17) | copy-start | bytes 1540
  662.9 201.9 %reduce-scatter.35.cloned.1.call-start = ((), (), s32[]{:S(2)}) async-start(), calls=%async_computation.27 | async-start | bytes 884736 | tf_op jit(solution)/shard_map/reduce_scatter | solution.py:274
  (24 other events, 440.5 us)
Sparse Core Ops, SparseCore 0:
  10.3 41.0 all-gather.23
  53.7 37.1 all-gather.25
  93.1 37.1 all-gather.21
  132.5 37.0 all-gather.27
  171.7 51.9 all-gather.29
  225.9 51.6 all-gather.31
  288.8 61.7 reduce-scatter.24
  354.3 62.1 reduce-scatter.12
  420.3 62.1 reduce-scatter.16
  486.2 62.2 reduce-scatter.20
  552.6 110.2 reduce-scatter.28
  666.8 112.7 reduce-scatter.32
  781.8 10.1 reduce-scatter.26
  794.1 10.5 reduce-scatter.14
  806.7 10.5 reduce-scatter.18
  819.3 10.5 reduce-scatter.22
  832.0 15.3 reduce-scatter.30
  849.5 15.3 reduce-scatter.34
where the time goes:
time: 887 us; the launch traced here: 885 us
  waiting for transfers between devices  555 us (63%)
  blocking collectives  210 us (24%)
  matrix products  58.7 us (7%)
  local copies, waits for them, and re-layouts  28.3 us (3%)
  between operations  20.1 us (2%)
    unnamed x4, blocking collectives  136 us
    reduce_scatter x1, waiting for transfers between devices, reduce_gradients(): lax.psum_scatter(gradients[11], 'fsdp', scatter_dimension=0, tiled=True)  110 us
    reduce_scatter x1, waiting for transfers between devices, reduce_gradients(): lax.psum_scatter(gradients[2], 'fsdp', scatter_dimension=0, tiled=True)  65.9 us
    reduce_scatter x1, waiting for transfers between devices, reduce_gradients(): lax.psum_scatter(gradients[4], 'fsdp', scatter_dimension=0, tiled=True)  62 us
    reduce_scatter x1, waiting for transfers between devices, reduce_gradients(): lax.psum_scatter(gradients[5], 'fsdp', scatter_dimension=0, tiled=True)  61.8 us
    all_gather x1, waiting for transfers between devices, gather_layer(): lax.all_gather(shards[11], 'fsdp', axis=0, tiled=True)  52.2 us
    all_gather x1, waiting for transfers between devices, gather_layer(): lax.all_gather(shards[13], 'fsdp', axis=0, tiled=True)  49.5 us
    reduce_scatter x1, waiting for transfers between devices, reduce_gradients(): lax.psum_scatter(gradients[13], 'fsdp', scatter_dimension=0, tiled=True)  44.5 us
  transfers between devices with their start and end apart: 19, of which 17 were waited for; matrix products, arithmetic and copies ran while one was open for 9% of the time, Pallas kernels for 0%

commit v1 on v0

--- a/solution.py
+++ b/solution.py
@@ -7,6 +7,28 @@
 EPSILON = 1e-05
 ROOT_HALF = 0.7071067811865476
 INV_ROOT_TAU = 0.3989422804014327
+
+
+def laid_out(pieces, dim):
+    shape = list(pieces.shape[1:])
+    shape[dim] *= pieces.shape[0]
+    return jnp.moveaxis(pieces, 0, dim).reshape(shape)
+
+
+def ring_gather(x, axis, dim):
+    peers = lax.axis_size(axis)
+    pairs = [(i, (i + 1) % peers) for i in range(peers)]
+    back = [(b, a) for a, b in pairs]
+    lower, upper = ([], [])
+    for step in range(peers - 1):
+        if step % 2 == 0:
+            lower.append(lax.ppermute(lower[-1] if lower else x, axis, pairs))
+        else:
+            upper.append(lax.ppermute(upper[-1] if upper else x, axis, back))
+    blocks = jnp.stack([*lower[::-1], x, *upper])
+    shift = lax.axis_index(axis) - len(lower)
+    blocks = blocks[(jnp.arange(peers) - shift) % peers]
+    return laid_out(blocks, dim)
 
 
 def matmul(left, right):
@@ -125,7 +147,7 @@
         lax.all_gather(shards[10], "fsdp", axis=0, tiled=True),
         lax.all_gather(shards[11], "fsdp", axis=0, tiled=True),
         lax.all_gather(shards[12], "fsdp", axis=0, tiled=True),
-        lax.all_gather(shards[13], "fsdp", axis=0, tiled=True),
+        ring_gather(shards[13], "fsdp", 0),
         lax.all_gather(shards[14], "fsdp", axis=0, tiled=True),
     )
 

time: 887 us -> 845 us (0.953)
  waiting for transfers between devices: 555 us -> 470 us
  starting transfers between devices: 4.15 us -> 37.9 us
  local copies, waits for them, and re-layouts: 28.3 us -> 50.6 us
  blocking collectives: 210 us -> 195 us
    all_gather x1 -> x0, waiting for transfers between devices: 49.5 us -> none  [gather_layer(): lax.all_gather(shards[13], 'fsdp', axis=0, tiled=True)]
    all_gather x1, waiting for transfers between devices: 37.9 us -> 0.02 us  [gather_layer(): lax.all_gather(shards[2], 'fsdp', axis=0, tiled=True)]
    ppermute x0 -> x15, starting transfers between devices: none -> 29.9 us  [the longest x7 27.9 us: ring_gather(): upper.append(lax.ppermute(upper[-1] if upper else x, axis, back))]
    ppermute x0 -> x15, waiting for transfers between devices: none -> 25.8 us  [the longest x8 21.5 us: ring_gather(): lower.append(lax.ppermute(lower[-1] if lower else x, axis, pairs))]
    all_gather x1, waiting for transfers between devices: 15.5 us -> 0.01 us  [gather_layer(): lax.all_gather(shards[7], 'fsdp', axis=0, tiled=True)]
    unnamed x110 -> x147, local copies, waits for them, and re-layouts: 18.6 us -> 32.9 us
    all_to_all x1 -> x0, blocking collectives: 13.9 us -> none  [forward_layer(): lax.all_to_all(jnp.stack([query_rows, key_rows, value_rows]), 'seq', spli...]
  transfers between devices with their start and end apart: 19 -> 34, of which waited for: 17 -> 22; matrix products, arithmetic and copies ran while one was open for 9% -> 12% of each run, Pallas kernels for 0% -> 0%
where the time goes in v1:
time: 845 us; the launch traced here: 843 us
  waiting for transfers between devices  470 us (56%)
  blocking collectives  195 us (23%)
  matrix products  57.7 us (7%)
  local copies, waits for them, and re-layouts  50.6 us (6%)
  starting transfers between devices  37.9 us (4%)
  between operations  19.9 us (2%)
  other arithmetic  11.3 us (1%)
    unnamed x4, blocking collectives  135 us
    reduce_scatter x1, waiting for transfers between devices, reduce_gradients(): lax.psum_scatter(gradients[11], 'fsdp', scatter_dimension=0, tiled=True)  110 us
    reduce_scatter x1, waiting for transfers between devices, reduce_gradients(): lax.psum_scatter(gradients[2], 'fsdp', scatter_dimension=0, tiled=True)  66 us
    reduce_scatter x1, waiting for transfers between devices, reduce_gradients(): lax.psum_scatter(gradients[4], 'fsdp', scatter_dimension=0, tiled=True)  62 us
    reduce_scatter x1, waiting for transfers between devices, reduce_gradients(): lax.psum_scatter(gradients[5], 'fsdp', scatter_dimension=0, tiled=True)  62 us
    all_gather x1, waiting for transfers between devices, gather_layer(): lax.all_gather(shards[11], 'fsdp', axis=0, tiled=True)  47.4 us
    reduce_scatter x1, waiting for transfers between devices, reduce_gradients(): lax.psum_scatter(gradients[13], 'fsdp', scatter_dimension=0, tiled=True)  44.8 us
    unnamed x147, local copies, waits for them, and re-layouts  32.9 us
  transfers between devices with their start and end apart: 34, of which 22 were waited for; matrix products, arithmetic and copies ran while one was open for 12% of the time, Pallas kernels for 0%

profile of v1, /device:TPU:0, one launch (start us, length us, event | category | flops | bytes accessed | tf_op | source)
XLA Modules:
  0.0 843.0 jit_solution(5659097234370245787)
XLA Ops:
  25.3 5.9 collective-permute-done.1
  69.0 62.3 %all-reduce.39 = (bf16[768]{0:T(1024)(128)(2,1)S(1)}, bf16[768]{0:T(1024)(128)(2,1)S(1)}, bf16[768]{0:T(1024)(128)(2,1)S(1)}, bf16[768]{0:T(1024)(128)(2,1)S(1)}...) all-reduce(bf16[768]{0:T(1024)(128)(2,1)S(1)} %dynamic-update-slice, ...), channel_id=3, replica_groups=mesh['seq'=2,'fsdp'=16] {'fsdp'}, use_global_device_ids=true, to_apply=%add.1 | all-reduce | flops 9216 | bytes 36864
  177.1 5.5 gather_fusion
  184.6 47.4 %all-gather.28.cloned.1.call-done = bf16[1,768,3072]{2,1,0:T(8,128)(2,1)} async-done(((bf16[1,48,3072]{2,1,0:T(8,128)(2,1)}), bf16[1,768,3072]{2,1,0:T(8,128)(2,1)}) %all-gather.28.cloned.1.call-update) | async-done | bytes 4718608 | tf_op jit(solution)/shard_map/all_gather | solution.py:148
  235.4 5.3 fusion.98
  248.3 7.5 all_to_all.62
  273.9 12.9 %all_to_all.63 = bf16[3,256,384]{2,0,1:T(4,128)(2,1)S(1)} all-to-all(bf16[3,256,384]{2,0,1:T(4,128)(2,1)S(1)} %pad_maximum_fusion), channel_id=1, replica_groups=mesh['seq'=2,'fsdp'=16] {'seq'}, dimensions={1} | all-to-all | bytes 1179648 | tf_op jit(solution)/shard_map/all_to_all | solution.py:225
  308.4 66.0 %reduce-scatter.13.cloned.1.call-done = f32[48,768]{1,0:T(8,128)} async-done(((f32[768,768]{1,0:T(8,128)}), f32[48,768]{1,0:T(8,128)}) %reduce-scatter.13.cloned.1.call-update) | async-done | bytes 147472 | tf_op jit(solution)/shard_map/reduce_scatter | solution.py:268
  378.3 62.0 %reduce-scatter.17.cloned.1.call-done = f32[48,768]{1,0:T(8,128)} async-done(((f32[768,768]{1,0:T(8,128)}), f32[48,768]{1,0:T(8,128)}) %reduce-scatter.17.cloned.1.call-update) | async-done | bytes 147472 | tf_op jit(solution)/shard_map/reduce_scatter | solution.py:270
  444.4 62.0 %reduce-scatter.21.cloned.1.call-done = f32[48,768]{1,0:T(8,128)} async-done(((f32[768,768]{1,0:T(8,128)}), f32[48,768]{1,0:T(8,128)}) %reduce-scatter.21.cloned.1.call-update) | async-done | bytes 147472 | tf_op jit(solution)/shard_map/reduce_scatter | solution.py:271
  510.6 110.0 %reduce-scatter.29.cloned.1.call-done = f32[48,3072]{1,0:T(8,128)} async-done(((f32[768,3072]{1,0:T(8,128)}), f32[48,3072]{1,0:T(8,128)}) %reduce-scatter.29.cloned.1.call-update) | async-done | bytes 589840 | tf_op jit(solution)/shard_map/reduce_scatter | solution.py:277
  623.6 62.3 %all-reduce.36 = (f32[768]{0:T(1024)S(1)}, f32[768]{0:T(1024)S(1)}, f32[768]{0:T(1024)S(1)}, f32[768]{0:T(1024)S(1)}, f32[768]{0:T(1024)S(1)}, /*index=5*/f32[76...) all-reduce(f32[768]{0:T(1024)S(1)} %get-tuple-element.19, ...), channel_id=16, replica_groups=mesh['seq'=2,'fsdp'=16] {'fsdp'}, use_global_device_ids=true, to_apply=%region_12.13.clone | all-reduce | flops 9216 | bytes 73728
  692.7 44.8 %reduce-scatter.33.cloned.1.call-done = f32[192,768]{1,0:T(8,128)} async-done(((f32[3072,768]{1,0:T(8,128)}), f32[192,768]{1,0:T(8,128)}) %reduce-scatter.33.cloned.1.call-update) | async-done | bytes 589840 | tf_op jit(solution)/shard_map/reduce_scatter | solution.py:279
  737.9 5.5 all-reduce.37
  744.3 5.4 reduce-scatter.27.cloned.1.call-done
  749.8 5.2 all_gather.108
  755.0 7.5 reduce-scatter.15.cloned.1.call-done
  762.5 5.2 all_gather.103
  767.8 7.4 reduce-scatter.19.cloned.1.call-done
  780.4 7.4 reduce-scatter.23.cloned.1.call-done
  793.0 12.3 %reduce-scatter.31.cloned.1.call-done = f32[24,3072]{1,0:T(8,128)} async-done(((f32[48,3072]{1,0:T(8,128)}), f32[24,3072]{1,0:T(8,128)}) %reduce-scatter.31.cloned.1.call-update) | async-done | bytes 294928 | tf_op jit(solution)/shard_map/reduce_scatter | solution.py:294
  805.3 9.5 %all_gather.112 = f32[48,3072]{1,0:T(8,128)S(1)} all-gather(f32[24,3072]{1,0:T(8,128)} %reduce-scatter.31.cloned.1.call-done), channel_id=1, replica_groups=mesh['seq'=2,'fsdp'=16] {'seq'}, dimensions={0}, use_global_device_ids=true | all-gather | bytes 884736 | tf_op jit(solution)/shard_map/all_gather | solution.py:311
  814.7 8.0 reduce-scatter.35.cloned.1.call-done
  822.8 9.5 %all_gather.114 = f32[192,768]{1,0:T(8,128)S(1)} all-gather(f32[96,768]{1,0:T(8,128)} %reduce-scatter.35.cloned.1.call-done), channel_id=1, replica_groups=mesh['seq'=2,'fsdp'=16] {'seq'}, dimensions={0}, use_global_device_ids=true | all-gather | bytes 884736 | tf_op jit(solution)/shard_map/all_gather | solution.py:313
  (299 shorter events, 186.3 us)
Async XLA Ops:
  7.2 135.9 %all-gather.24.cloned.1.call-start = ((), (), s32[]{:S(2)}) async-start(), calls=%async_computation.30 | async-start | bytes 1253376 | tf_op jit(solution)/shard_map/all_gather | solution.py:142
  7.9 136.9 %all-gather.20.cloned.1.call-start = ((), (), s32[]{:S(2)}) async-start(), calls=%async_computation.28 | async-start | bytes 1253376 | tf_op jit(solution)/shard_map/all_gather | solution.py:139
  8.7 137.9 %all-gather.22.cloned.1.call-start = ((), (), s32[]{:S(2)}) async-start(), calls=%async_computation.29 | async-start | bytes 1253376 | tf_op jit(solution)/shard_map/all_gather | solution.py:141
  9.4 173.2 %all-gather.26.cloned.1.call-start = ((), (), s32[]{:S(2)}) async-start(), calls=%async_computation.31 | async-start | bytes 1253376 | tf_op jit(solution)/shard_map/all_gather | solution.py:144
  10.0 222.0 %all-gather.28.cloned.1.call-start = ((), (), s32[]{:S(2)}) async-start(), calls=%async_computation.32 | async-start | bytes 5013504 | tf_op jit(solution)/shard_map/all_gather | solution.py:148
  20.8 10.4 %collective-permute-start.1 = (bf16[192,768]{1,0:T(8,128)(2,1)S(1)}, bf16[192,768]{1,0:T(8,128)(2,1)S(1)}, u32[]{:S(2)}, u32[]{:S(2)}) collective-permute-start(bf16[192,768]{1,0:T(8,128)(2,1)S(1)} %collective-permute-done), channel_id=1, source_target_pairs={{0,1},{1,2},{2,3},{3,4},{4,5},{5,6},{6,7},{7,8},{8,9},{9,10},{10,1... | collective-permute-start | bytes 884744 | tf_op jit(solution)/shard_map/ppermute | solution.py:25
  31.2 10.5 %collective-permute-start.10 = (bf16[192,768]{1,0:T(8,128)(2,1)S(1)}, bf16[192,768]{1,0:T(8,128)(2,1)S(1)}, u32[]{:S(2)}, u32[]{:S(2)}) collective-permute-start(bf16[192,768]{1,0:T(8,128)(2,1)S(1)} %collective-permute-done.9), channel_id=1, source_target_pairs={{1,0},{2,1},{3,2},{4,3},{5,4},{6,5},{7,6},{8,7},{9,8},{10,9},{11,1... | collective-permute-start | bytes 884744 | tf_op jit(solution)/shard_map/ppermute | solution.py:27
  51.2 82.5 %collective-permute-start.12 = (bf16[192,768]{1,0:T(8,128)(2,1)S(1)}, bf16[192,768]{1,0:T(8,128)(2,1)S(1)}, u32[]{:S(2)}, u32[]{:S(2)}) collective-permute-start(bf16[192,768]{1,0:T(8,128)(2,1)S(1)} %collective-permute-done.11), channel_id=1, source_target_pairs={{1,0},{2,1},{3,2},{4,3},{5,4},{6,5},{7,6},{8,7},{9,8},{10,9},{11,1... | collective-permute-start | bytes 884744 | tf_op jit(solution)/shard_map/ppermute | solution.py:27
  58.7 75.1 %collective-permute-start.5 = (bf16[192,768]{1,0:T(8,128)(2,1)S(1)}, bf16[192,768]{1,0:T(8,128)(2,1)}, u32[]{:S(2)}, u32[]{:S(2)}) collective-permute-start(bf16[192,768]{1,0:T(8,128)(2,1)S(1)} %collective-permute-done.4), channel_id=1, source_target_pairs={{0,1},{1,2},{2,3},{3,4},{4,5},{5,6},{6,7},{7,8},{8,9},{9,10},{10,1... | collective-permute-start | bytes 884744 | tf_op jit(solution)/shard_map/ppermute | solution.py:25
  138.1 37.2 %collective-permute-start.14 = (bf16[192,768]{1,0:T(8,128)(2,1)}, bf16[192,768]{1,0:T(8,128)(2,1)}, u32[]{:S(2)}, u32[]{:S(2)}) collective-permute-start(bf16[192,768]{1,0:T(8,128)(2,1)} %collective-permute-done.13), channel_id=1, source_target_pairs={{1,0},{2,1},{3,2},{4,3},{5,4},{6,5},{7,6},{8,7},{9,8},{10,9},{11,1... | collective-permute-start | bytes 884744 | tf_op jit(solution)/shard_map/ppermute | solution.py:27
  149.6 18.7 %all-to-all-start = ((bf16[3,128,768]{1,0,2:T(4,128)(2,1)}), bf16[3,128,768]{1,0,2:T(4,128)(2,1)S(1)}, u32[]{:S(2)}, u32[]{:S(2)}) async-start(bf16[3,128,768]{1,0,2:T(4,128)(2,1)} %copy.66), calls=%async_computation | async-start | bytes 1572864 | tf_op jit(solution)/shard_map/all_to_all | solution.py:161
  171.7 10.9 %all-to-all-start.1 = ((bf16[2,128,384]{1,2,0:T(8,128)(2,1)}), bf16[2,128,384]{1,2,0:T(8,128)(2,1)S(1)}, u32[]{:S(2)}, u32[]{:S(2)}) async-start(bf16[2,128,384]{1,2,0:T(8,128)(2,1)} %copy.69), calls=%async_computation.1 | async-start | bytes 393216 | tf_op jit(solution)/shard_map/all_to_all | solution.py:169
  175.1 133.2 %reduce-scatter.25.cloned.1.call-start = ((), (), s32[]{:S(2)}) async-start(), calls=%async_computation.22 | async-start | bytes 2506752 | tf_op jit(solution)/shard_map/reduce_scatter | solution.py:273
  246.4 127.9 %reduce-scatter.13.cloned.1.call-start = ((), (), s32[]{:S(2)}) async-start(), calls=%async_computation.16 | async-start | bytes 2506752 | tf_op jit(solution)/shard_map/reduce_scatter | solution.py:268
  290.0 150.4 %reduce-scatter.17.cloned.1.call-start = ((), (), s32[]{:S(2)}) async-start(), calls=%async_computation.18 | async-start | bytes 2506752 | tf_op jit(solution)/shard_map/reduce_scatter | solution.py:270
  292.3 214.1 %reduce-scatter.21.cloned.1.call-start = ((), (), s32[]{:S(2)}) async-start(), calls=%async_computation.20 | async-start | bytes 2506752 | tf_op jit(solution)/shard_map/reduce_scatter | solution.py:271
  294.6 326.0 %reduce-scatter.29.cloned.1.call-start = ((), (), s32[]{:S(2)}) async-start(), calls=%async_computation.24 | async-start | bytes 10027008 | tf_op jit(solution)/shard_map/reduce_scatter | solution.py:277
  300.9 436.6 %reduce-scatter.33.cloned.1.call-start = ((), (), s32[]{:S(2)}) async-start(), calls=%async_computation.26 | async-start | bytes 10027008 | tf_op jit(solution)/shard_map/reduce_scatter | solution.py:279
  307.4 442.4 %reduce-scatter.27.cloned.1.call-start = ((), (), s32[]{:S(2)}) async-start(), calls=%async_computation.23 | async-start | bytes 221184 | tf_op jit(solution)/shard_map/reduce_scatter | solution.py:290
  308.3 454.2 %reduce-scatter.15.cloned.1.call-start = ((), (), s32[]{:S(2)}) async-start(), calls=%async_computation.17 | async-start | bytes 221184 | tf_op jit(solution)/shard_map/reduce_scatter | solution.py:285
  374.4 400.8 %reduce-scatter.19.cloned.1.call-start = ((), (), s32[]{:S(2)}) async-start(), calls=%async_computation.19 | async-start | bytes 221184 | tf_op jit(solution)/shard_map/reduce_scatter | solution.py:287
  440.4 347.4 %reduce-scatter.23.cloned.1.call-start = ((), (), s32[]{:S(2)}) async-start(), calls=%async_computation.21 | async-start | bytes 221184 | tf_op jit(solution)/shard_map/reduce_scatter | solution.py:288
  506.4 298.9 %reduce-scatter.31.cloned.1.call-start = ((), (), s32[]{:S(2)}) async-start(), calls=%async_computation.25 | async-start | bytes 884736 | tf_op jit(solution)/shard_map/reduce_scatter | solution.py:294
  620.7 202.1 %reduce-scatter.35.cloned.1.call-start = ((), (), s32[]{:S(2)}) async-start(), calls=%async_computation.27 | async-start | bytes 884736 | tf_op jit(solution)/shard_map/reduce_scatter | solution.py:296
  (50 other events, 1279.8 us)
Sparse Core Ops, SparseCore 0:
  10.3 44.9 all-gather.23
  57.5 37.3 all-gather.19
  97.2 39.5 all-gather.21
  138.9 38.8 all-gather.25
  180.0 51.9 all-gather.27
  246.5 61.7 reduce-scatter.24
  312.1 62.2 reduce-scatter.12
  378.1 62.2 reduce-scatter.16
  444.1 62.2 reduce-scatter.20
  510.3 110.2 reduce-scatter.28
  624.7 112.7 reduce-scatter.32
  739.6 10.1 reduce-scatter.26
  752.0 10.5 reduce-scatter.14
  764.6 10.5 reduce-scatter.18
  777.2 10.5 reduce-scatter.22
  789.9 15.3 reduce-scatter.30
  807.4 15.3 reduce-scatter.34
